TPU v7x, 256 devices: a whole 4x4x8 slice. The times are simulated.
256 devices in a mesh: seq: 32 (over z, y_lo, core), tp: 8 (over x, y_hi).
Axes of the slice: x: 4, y: 4 (y_hi: 2, y_lo: 2; y = y_hi * 2 + y_lo), z: 8, core: 2. Of those that a mesh axis runs over, the one named last changes fastest.
Arguments:
- grad_out: bfloat16 [8192, 14336], P('seq', 'tp'), may hold values from -6 to 6
- weight: bfloat16 [4096, 14336], P('seq', 'tp'), may hold values from -0.046875 to 0.046875
- saved: bfloat16 [8192, 512], P('seq'), may hold values from -0.125 to 0.125
- first_moment: float32 [512, 14336], P('seq', 'tp'), may hold values from -6 to 6
- second_moment: float32 [512, 14336], P('seq', 'tp'), may hold values from 0.05 to 2
- basis: bfloat16 [4096, 512], P('seq'), may hold values from -0.0625 to 0.0625
- new_basis: bfloat16 [4096, 512], P('seq'), may hold values from -0.09375 to 0.09375
Outputs:
- grad_input: float32 [8192, 4096], P('seq', 'tp')
- first_new: float32 [512, 14336], P('seq', 'tp')
- second_new: float32 [512, 14336], P('seq', 'tp')
- update: float32 [512, 14336], P('seq', 'tp')
All inputs are finite; a program needn't handle non-finite values.
Results may differ from a plain program's by a relative error of at most 0.0003.
Values may be sent and summed in bfloat16 or wider, within the bound.
A program may use at most 128 MiB of HBM per device.

v0:
```python
import jax
import jax.numpy as jnp
from jax import lax
from jax.sharding import PartitionSpec as P


def contract_rows(left, right):
    return lax.dot_general(
        left, right, (((0,), (0,)), ((), ())), preferred_element_type=jnp.float32
    )


def exact_dot(left, right):
    return jnp.dot(left, right, precision=lax.Precision.HIGHEST, preferred_element_type=jnp.float32)


def per_device(grad_out, weight, saved, first_moment, second_moment, basis, new_basis):
    rank_rows = first_moment.shape[0]
    row_start = lax.axis_index("seq") * rank_rows
    partial_input = lax.dot_general(
        grad_out,
        lax.all_gather(weight, "seq", axis=0, tiled=True),
        (((1,), (1,)), ((), ())),
        preferred_element_type=jnp.float32,
    )
    grad_input = lax.psum_scatter(partial_input, "tp", scatter_dimension=1, tiled=True)
    local_intersection = contract_rows(new_basis, basis)
    intersection = lax.psum(local_intersection, "seq")
    gradient = lax.psum_scatter(
        contract_rows(saved, grad_out), "seq", scatter_dimension=0, tiled=True
    )
    full_first, full_second = (
        lax.all_gather(first_moment, "seq", axis=0, tiled=True),
        lax.all_gather(second_moment, "seq", axis=0, tiled=True),
    )
    own_rows = lax.dynamic_slice_in_dim(intersection, row_start, rank_rows, 0)
    first_rot = exact_dot(own_rows, full_first)
    second_rot = exact_dot(own_rows * own_rows, full_second)
    first_new = 0.9 * first_rot + 0.1 * gradient
    second_new = 0.95 * second_rot + 0.05 * gradient * gradient
    update = first_new / (jnp.sqrt(second_new) + 1e-08)
    return (grad_input, first_new, second_new, update)


def solution(mesh):
    return jax.shard_map(
        per_device,
        mesh=mesh,
        in_specs=(
            P("seq", "tp"),
            P("seq", "tp"),
            P("seq", None),
            P("seq", "tp"),
            P("seq", "tp"),
            P("seq", None),
            P("seq", None),
        ),
        out_specs=(P("seq", "tp"), P("seq", "tp"), P("seq", "tp"), P("seq", "tp")),
        check_vma=False,
    )
```

profile of v0, /device:TPU:2, one launch (start us, length us, event | category | flops | bytes accessed | tf_op | source)
XLA Modules:
  0.0 695.8 jit_solution(15503047025166529226)
XLA Ops:
  7.2 0.0 copy-start
  7.2 0.0 all-gather.4.cloned.1.call-start
  7.2 0.7 all-gather.4.cloned.1.call-update
  7.9 0.0 all-reduce.2.cloned.1.call-start
  8.0 2.2 fusion.8
  10.2 0.0 all-reduce.2.cloned.1.call-update
  10.2 0.0 all-gather.8.cloned.1.call-start
  10.3 0.7 all-gather.8.cloned.1.call-update
  11.0 0.0 reduce-scatter.5.cloned.1.call-start
  11.0 0.0 copy-done
  11.0 3.5 fusion.9
  14.5 0.0 reduce-scatter.5.cloned.1.call-update
  14.5 0.0 all-gather.6.cloned.1.call-start
  14.6 0.5 all-gather.6.cloned.1.call-update
  15.1 0.0 reduce-scatter.3.cloned.1.call-start
  15.2 86.8 %all-gather.4.cloned.1.call-done = bf16[4096,1792]{1,0:T(8,128)(2,1)} async-done(((bf16[128,1792]{1,0:T(8,128)(2,1)}), bf16[4096,1792]{1,0:T(8,128)(2,1)}) %all-gather.4.cloned.1.call-update) | async-done | bytes 14680080 | tf_op jit(solution)/shard_map/all_gather | solution.py:22
  102.0 16.0 %fusion.7 = f32[256,4096]{1,0:T(8,128)} fusion(bf16[256,1792]{1,0:T(8,128)(2,1)S(1)} %copy-done, bf16[4096,1792]{1,0:T(8,128)(2,1)} %all-gather.4.cloned.1.call-done), kind=kOutput, calls=%fused_computation.11 | convolution fusion | flops 3758096384 | bytes 19791872 | tf_op jit(solution)/shard_map/dot_general | solution.py:20
  118.0 0.0 reduce-scatter.3.cloned.1.call-update
  118.0 216.1 %all-reduce.2.cloned.1.call-done = f32[512,512]{1,0:T(8,128)} async-done(((f32[512,512]{1,0:T(8,128)}), f32[512,512]{1,0:T(8,128)}) %all-reduce.2.cloned.1.call-update) | async-done | bytes 1048592 | tf_op jit(solution)/shard_map/psum | solution.py:28
  334.1 68.7 %all-gather.8.cloned.1.call-done = f32[512,1792]{1,0:T(8,128)} async-done(((f32[16,1792]{1,0:T(8,128)}), f32[512,1792]{1,0:T(8,128)}) %all-gather.8.cloned.1.call-update) | async-done | bytes 3670032 | tf_op jit(solution)/shard_map/all_gather | solution.py:34
  402.7 125.6 %reduce-scatter.5.cloned.1.call-done = f32[16,1792]{1,0:T(8,128)} async-done(((f32[512,1792]{1,0:T(8,128)}), f32[16,1792]{1,0:T(8,128)}) %reduce-scatter.5.cloned.1.call-update) | async-done | bytes 114704 | tf_op jit(solution)/shard_map/reduce_scatter | solution.py:29
  528.3 0.0 copy-start.1
  528.3 3.8 fusion
  532.2 0.0 copy-start.2
  532.2 62.1 %all-gather.6.cloned.1.call-done = f32[512,1792]{1,0:T(8,128)} async-done(((f32[16,1792]{1,0:T(8,128)}), f32[512,1792]{1,0:T(8,128)}) %all-gather.6.cloned.1.call-update) | async-done | bytes 3670032 | tf_op jit(solution)/shard_map/all_gather | solution.py:33
  594.3 0.0 copy-done.1
  594.3 4.5 add_divide_fusion
  598.9 90.0 %reduce-scatter.3.cloned.1.call-done = f32[256,512]{1,0:T(8,128)} async-done(((f32[256,4096]{1,0:T(8,128)}), f32[256,512]{1,0:T(8,128)}) %reduce-scatter.3.cloned.1.call-update) | async-done | bytes 524304 | tf_op jit(solution)/shard_map/reduce_scatter | solution.py:26
  688.9 0.0 copy-done.2
Async XLA Ops:
  7.2 3.8 copy-start
  7.2 94.8 %all-gather.4.cloned.1.call-start = ((), (), s32[]{:S(2)}) async-start(), calls=%async_computation.2 | async-start | bytes 15138816 | tf_op jit(solution)/shard_map/all_gather | solution.py:22
  7.9 326.1 %all-reduce.2.cloned.1.call-start = ((), (), s32[]{:S(2)}) async-start(), calls=%async_computation.4 | async-start | bytes 2097152 | tf_op jit(solution)/shard_map/psum | solution.py:28
  10.2 392.5 %all-gather.8.cloned.1.call-start = ((), (), s32[]{:S(2)}) async-start(), calls=%async_computation.7 | async-start | bytes 3784704 | tf_op jit(solution)/shard_map/all_gather | solution.py:34
  11.0 517.4 %reduce-scatter.5.cloned.1.call-start = ((), (), s32[]{:S(2)}) async-start(), calls=%async_computation.6 | async-start | bytes 3784704 | tf_op jit(solution)/shard_map/reduce_scatter | solution.py:29
  14.5 579.8 %all-gather.6.cloned.1.call-start = ((), (), s32[]{:S(2)}) async-start(), calls=%async_computation.5 | async-start | bytes 3784704 | tf_op jit(solution)/shard_map/all_gather | solution.py:33
  15.1 673.8 %reduce-scatter.3.cloned.1.call-start = ((), (), s32[]{:S(2)}) async-start(), calls=%async_computation.3 | async-start | bytes 4718592 | tf_op jit(solution)/shard_map/reduce_scatter | solution.py:26
  528.3 66.0 %copy-start.1 = (f32[16,1792]{1,0:T(8,128)S(1)}, f32[16,1792]{1,0:T(8,128)}, u32[]{:S(2)}) copy-start(f32[16,1792]{1,0:T(8,128)} %reduce-scatter.5.cloned.1.call-done) | copy-start | bytes 344068
  532.2 156.7 %copy-start.2 = (f32[16,1792]{1,0:T(8,128)}, f32[16,1792]{1,0:T(8,128)S(1)}, u32[]{:S(2)}) copy-start(f32[16,1792]{1,0:T(8,128)S(1)} %fusion) | copy-start | bytes 344068
Sparse Core Ops, SparseCore 0:
  9.8 92.0 all-gather.3
  104.6 229.4 all-reduce.1
  335.9 66.7 all-gather.7
  405.1 123.1 reduce-scatter.4
  530.0 64.2 all-gather.5
  598.9 89.9 reduce-scatter.2
where the time goes:
time: 696 us
  waiting for transfers between devices  651 us (94%)
  matrix products  30.1 us (4%)
  between operations  14.1 us (2%)
    psum x1, waiting for transfers between devices, per_device(): intersection = lax.psum(local_intersection, 'seq')  216 us
    reduce_scatter x1, waiting for transfers between devices, per_device(): lax.psum_scatter(contract_rows(saved, grad_out), 'seq', scatter_dimension...  126 us
    reduce_scatter x1, waiting for transfers between devices, per_device(): lax.psum_scatter(partial_input, 'tp', scatter_dimension=1, tiled=True)  90 us
    all_gather x1, waiting for transfers between devices, per_device(): lax.all_gather(weight, 'seq', axis=0, tiled=True)  86.8 us
    all_gather x1, waiting for transfers between devices, per_device(): lax.all_gather(second_moment, 'seq', axis=0, tiled=True)  68.7 us
    all_gather x1, waiting for transfers between devices, per_device(): lax.all_gather(first_moment, 'seq', axis=0, tiled=True)  62.1 us
    dot_general x1, matrix products, per_device(): lax.dot_general(grad_out, lax.all_gather(weight, 'seq', axis=0, tiled=Tru...  16 us
  transfers between devices with their start and end apart: 6, of which 6 were waited for; matrix products, arithmetic and copies ran while one was open for 4% of the time, Pallas kernels for 0%

commit v1 on v0

--- a/solution.py
+++ b/solution.py
@@ -2,6 +2,11 @@
 import jax.numpy as jnp
 from jax import lax
 from jax.sharding import PartitionSpec as P
+
+
+def swapped_in(x, name, dim):
+    sent = jnp.stack([x] * lax.axis_size(name))
+    return jnp.concatenate(lax.all_to_all(sent, name, 0, 0), axis=dim)
 
 
 def contract_rows(left, right):
@@ -30,7 +35,7 @@
         contract_rows(saved, grad_out), "seq", scatter_dimension=0, tiled=True
     )
     full_first, full_second = (
-        lax.all_gather(first_moment, "seq", axis=0, tiled=True),
+        swapped_in(first_moment, "seq", 0),
         lax.all_gather(second_moment, "seq", axis=0, tiled=True),
     )
     own_rows = lax.dynamic_slice_in_dim(intersection, row_start, rank_rows, 0)

time: 696 us -> 649 us (0.932)
  waiting for transfers between devices: 651 us -> 594 us
  starting transfers between devices: 0.24 us -> 7.65 us
    all_gather x1 -> x0, waiting for transfers between devices: 62.1 us -> none  [per_device(): lax.all_gather(first_moment, 'seq', axis=0, tiled=True)]
    psum x1, waiting for transfers between devices: 216 us -> 226 us  [per_device(): intersection = lax.psum(local_intersection, 'seq')]
    all_to_all x0 -> x1, starting transfers between devices: none -> 7.46 us  [swapped_in(): return jnp.concatenate(lax.all_to_all(sent, name, 0, 0), axis=dim)]
  transfers between devices with their start and end apart: 6 -> 6, of which waited for: 6 -> 5; matrix products, arithmetic and copies ran while one was open for 4% -> 5% of each run, Pallas kernels for 0% -> 0%
where the time goes in v1:
time: 649 us; the launch traced here: 648 us
  waiting for transfers between devices  594 us (92%)
  matrix products  30.2 us (5%)
  between operations  13.8 us (2%)
  starting transfers between devices  7.65 us (1%)
    psum x1, waiting for transfers between devices, per_device(): intersection = lax.psum(local_intersection, 'seq')  226 us
    reduce_scatter x1, waiting for transfers between devices, per_device(): lax.psum_scatter(contract_rows(saved, grad_out), 'seq', scatter_dimension...  126 us
    all_gather x1, waiting for transfers between devices, per_device(): lax.all_gather(weight, 'seq', axis=0, tiled=True)  87.3 us
    reduce_scatter x1, waiting for transfers between devices, per_device(): lax.psum_scatter(partial_input, 'tp', scatter_dimension=1, tiled=True)  84.7 us
    all_gather x1, waiting for transfers between devices, per_device(): lax.all_gather(second_moment, 'seq', axis=0, tiled=True)  68.7 us
    dot_general x1, matrix products, per_device(): lax.dot_general(grad_out, lax.all_gather(weight, 'seq', axis=0, tiled=Tru...  16 us
  transfers between devices with their start and end apart: 6, of which 5 were waited for; matrix products, arithmetic and copies ran while one was open for 5% of the time, Pallas kernels for 0%

profile of v1, /device:TPU:2, one launch (start us, length us, event | category | flops | bytes accessed | tf_op | source)
XLA Modules:
  0.0 648.3 jit_solution(3584036406594591965)
XLA Ops:
  7.2 0.0 copy-start
  7.2 0.0 all-gather.3.cloned.1.call-start
  7.2 0.7 all-gather.3.cloned.1.call-update
  7.9 0.0 all-reduce.2.cloned.1.call-start
  8.0 2.3 fusion.8
  10.2 0.0 all-reduce.2.cloned.1.call-update
  10.2 0.0 all-gather.5.cloned.1.call-start
  10.3 0.7 all-gather.5.cloned.1.call-update
  11.0 0.0 reduce-scatter.5.cloned.1.call-start
  11.0 0.0 copy-done
  11.0 3.5 fusion.9
  14.5 0.0 reduce-scatter.5.cloned.1.call-update
  14.6 0.0 reduce-scatter.3.cloned.1.call-start
  14.6 87.3 %all-gather.3.cloned.1.call-done = bf16[4096,1792]{1,0:T(8,128)(2,1)} async-done(((bf16[128,1792]{1,0:T(8,128)(2,1)}), bf16[4096,1792]{1,0:T(8,128)(2,1)}) %all-gather.3.cloned.1.call-update) | async-done | bytes 14680080 | tf_op jit(solution)/shard_map/all_gather | solution.py:27
  102.0 16.0 %fusion.7 = f32[256,4096]{1,0:T(8,128)} fusion(bf16[256,1792]{1,0:T(8,128)(2,1)S(1)} %copy-done, bf16[4096,1792]{1,0:T(8,128)(2,1)} %all-gather.3.cloned.1.call-done), kind=kOutput, calls=%fused_computation.11 | convolution fusion | flops 3758096384 | bytes 19791872 | tf_op jit(solution)/shard_map/dot_general | solution.py:25
  118.0 0.0 copy-start.3
  118.0 0.0 reduce-scatter.3.cloned.1.call-update
  118.0 0.9 copy-done.3
  118.9 2.3 stack.2
  121.1 7.5 %all-to-all-start = ((f32[32,16,1792]{2,1,0:T(8,128)}), f32[32,16,1792]{2,1,0:T(8,128)}, u32[]{:S(2)}, u32[]{:S(2)}) async-start(f32[32,16,1792]{2,1,0:T(8,128)} %stack.2), calls=%async_computation.1 | async-start | bytes 7340032 | tf_op jit(solution)/shard_map/all_to_all | solution.py:9
  128.6 225.8 %all-reduce.2.cloned.1.call-done = f32[512,512]{1,0:T(8,128)} async-done(((f32[512,512]{1,0:T(8,128)}), f32[512,512]{1,0:T(8,128)}) %all-reduce.2.cloned.1.call-update) | async-done | bytes 1048592 | tf_op jit(solution)/shard_map/psum | solution.py:33
  354.4 68.7 %all-gather.5.cloned.1.call-done = f32[512,1792]{1,0:T(8,128)} async-done(((f32[16,1792]{1,0:T(8,128)}), f32[512,1792]{1,0:T(8,128)}) %all-gather.5.cloned.1.call-update) | async-done | bytes 3670032 | tf_op jit(solution)/shard_map/all_gather | solution.py:39
  423.0 125.6 %reduce-scatter.5.cloned.1.call-done = f32[16,1792]{1,0:T(8,128)} async-done(((f32[512,1792]{1,0:T(8,128)}), f32[16,1792]{1,0:T(8,128)}) %reduce-scatter.5.cloned.1.call-update) | async-done | bytes 114704 | tf_op jit(solution)/shard_map/reduce_scatter | solution.py:34
  548.7 0.0 copy-start.1
  548.7 3.8 fusion
  552.5 0.0 copy-start.2
  552.5 0.0 all-to-all-done
  552.5 0.0 copy-done.1
  552.6 4.6 add_divide_fusion
  557.1 84.7 %reduce-scatter.3.cloned.1.call-done = f32[256,512]{1,0:T(8,128)} async-done(((f32[256,4096]{1,0:T(8,128)}), f32[256,512]{1,0:T(8,128)}) %reduce-scatter.3.cloned.1.call-update) | async-done | bytes 524304 | tf_op jit(solution)/shard_map/reduce_scatter | solution.py:31
  641.8 0.0 copy-done.2
Async XLA Ops:
  7.2 3.9 copy-start
  7.2 94.8 %all-gather.3.cloned.1.call-start = ((), (), s32[]{:S(2)}) async-start(), calls=%async_computation.3 | async-start | bytes 15138816 | tf_op jit(solution)/shard_map/all_gather | solution.py:27
  7.9 346.5 %all-reduce.2.cloned.1.call-start = ((), (), s32[]{:S(2)}) async-start(), calls=%async_computation.5 | async-start | bytes 2097152 | tf_op jit(solution)/shard_map/psum | solution.py:33
  10.2 412.8 %all-gather.5.cloned.1.call-start = ((), (), s32[]{:S(2)}) async-start(), calls=%async_computation.7 | async-start | bytes 3784704 | tf_op jit(solution)/shard_map/all_gather | solution.py:39
  11.0 537.7 %reduce-scatter.5.cloned.1.call-start = ((), (), s32[]{:S(2)}) async-start(), calls=%async_computation.6 | async-start | bytes 3784704 | tf_op jit(solution)/shard_map/reduce_scatter | solution.py:34
  14.6 627.2 %reduce-scatter.3.cloned.1.call-start = ((), (), s32[]{:S(2)}) async-start(), calls=%async_computation.4 | async-start | bytes 4718592 | tf_op jit(solution)/shard_map/reduce_scatter | solution.py:31
  118.0 0.9 copy-start.3
  121.1 431.4 %all-to-all-start = ((f32[32,16,1792]{2,1,0:T(8,128)}), f32[32,16,1792]{2,1,0:T(8,128)}, u32[]{:S(2)}, u32[]{:S(2)}) async-start(f32[32,16,1792]{2,1,0:T(8,128)} %stack.2), calls=%async_computation.1 | async-start | bytes 7340032 | tf_op jit(solution)/shard_map/all_to_all | solution.py:9
  548.7 3.9 copy-start.1
  552.5 89.3 %copy-start.2 = (f32[16,1792]{1,0:T(8,128)}, f32[16,1792]{1,0:T(8,128)S(1)}, u32[]{:S(2)}) copy-start(f32[16,1792]{1,0:T(8,128)S(1)} %fusion) | copy-start | bytes 344068
Sparse Core Ops, SparseCore 0:
  9.8 92.0 all-gather.2
  104.6 249.7 all-reduce.1
  356.3 66.7 all-gather.4
  425.4 123.1 reduce-scatter.4
  553.3 88.4 reduce-scatter.2
